TPU v7x, 256 devices: a whole 4x4x8 slice. The times are simulated.
256 devices in a mesh: expert: 4 (over z_lo), etp: 16 (over y, x), tp: 4 (over z_hi, core).
Axes of the slice: x: 4, y: 4, z: 8 (z_hi: 2, z_lo: 4; z = z_hi * 4 + z_lo), core: 2. Of those that a mesh axis runs over, the one named last changes fastest.
Arguments:
- d_out: bfloat16 [2048, 6144], P(('expert', 'tp'), 'etp'), may hold values from -6 to 6
- expert_ids: int32 [2048, 2], P(('expert', 'tp')), may hold values from 0 to 3, all different within a row; in each aligned block of 128 rows (0 to 127, 128 to 255, ...) at most 64 rows name the same one
- gate_weights: float32 [2048, 2], P(('expert', 'tp')), may hold values from 0.05 to 0.95, as said below
- saved_gate: bfloat16 [4, 1024, 16384], P('expert', None, ('etp', 'tp')), may hold values from -8 to 8
- saved_up: bfloat16 [4, 1024, 16384], P('expert', None, ('etp', 'tp')), may hold values from -6 to 6
- w_gate: bfloat16 [4, 6144, 16384], P('expert', None, ('etp', 'tp')), may hold values from -0.078125 to 0.078125
- w_up: bfloat16 [4, 6144, 16384], P('expert', None, ('etp', 'tp')), may hold values from -0.078125 to 0.078125
- w_down: bfloat16 [4, 16384, 6144], P('expert', ('etp', 'tp')), may hold values from -0.046875 to 0.046875
- w_out: bfloat16 [6144, 6144], P('tp', 'etp'), may hold values from -0.078125 to 0.078125
Outputs:
- d_hidden: bfloat16 [2048, 6144], P(('expert', 'tp'), 'etp')
- d_heads: bfloat16 [2048, 6144], P(('expert', 'etp'), 'tp')
Inputs may be any that keep to these rules, and one draw needn't show every extreme that they name: `expert_ids`: each token names two different experts; in every block of 128 tokens every expert is named by exactly 64 tokens. `gate_weights`: a token's two weights sum to one.
All inputs are finite; a program needn't handle non-finite values.
Results may differ from a plain program's by a relative error of at most 0.02.
Values may be sent and summed in bfloat16 or wider, within the bound.
No kernel may reach another device: no remote copies, remote signals or barrier semaphores. Data moves between devices by JAX's collectives and lax.ppermute only.
A program may use at most 128 MiB of HBM per device.

v0:
```python
import jax
import jax.numpy as jnp
from jax import lax
from jax.sharding import PartitionSpec as P


def body(d_out, expert_ids, gate_weights, saved_gate, saved_up, w_gate, w_up, w_down, w_out):
    expert_count = lax.axis_size("expert")
    tp_count = lax.axis_size("tp")
    feat_local = d_out.shape[1]
    cap_slots = saved_gate.shape[1] // (expert_count * tp_count)
    model_width = w_gate.shape[1]
    experts_iota = jnp.arange(expert_count, dtype=jnp.int32)
    first_hit = expert_ids[:, 0:1] == experts_iota[None, :]
    second_hit = expert_ids[:, 1:2] == experts_iota[None, :]
    member = first_hit.astype(jnp.int32) + second_hit.astype(jnp.int32)
    weight = gate_weights[:, 0:1] * first_hit.astype(jnp.float32) + gate_weights[
        :, 1:2
    ] * second_hit.astype(jnp.float32)
    slot = jnp.cumsum(member, axis=0) - member
    slot_iota = jnp.arange(cap_slots, dtype=jnp.int32)
    select = ((slot[:, :, None] == slot_iota[None, None, :]) & (member[:, :, None] > 0)).astype(
        jnp.float32
    )
    weighted_sel = select * weight[:, :, None]
    outgoing = jnp.einsum(
        "tec,td->ecd", weighted_sel, d_out.astype(jnp.float32), precision=lax.Precision.HIGHEST
    ).astype(jnp.bfloat16)
    received = lax.all_to_all(outgoing, "expert", split_axis=0, concat_axis=0, tiled=True)
    blocks_all = lax.all_gather(received[:, None], "tp", axis=1, tiled=True)
    down_local = w_down[0]
    slot_rows = blocks_all.shape[0] * blocks_all.shape[1] * blocks_all.shape[2]
    shard_piece = lax.all_gather(blocks_all, "etp", axis=3, tiled=True)
    width_piece = shard_piece.shape[3]
    flat_rows = shard_piece.reshape(slot_rows, width_piece)
    grad_act = lax.dot_general(
        flat_rows, down_local, (((1,), (1,)), ((), ())), preferred_element_type=jnp.float32
    )
    gate_val = saved_gate[0].astype(jnp.float32)
    up_val = saved_up[0].astype(jnp.float32)
    sigma = jax.nn.sigmoid(gate_val)
    grad_up = (grad_act * gate_val * sigma).astype(jnp.bfloat16)
    grad_gate = (grad_act * up_val * sigma * (1.0 + gate_val * (1.0 - sigma))).astype(jnp.bfloat16)
    gate_local = w_gate[0]
    up_local = w_up[0]
    first_part = lax.dot_general(
        gate_local, grad_gate, (((1,), (1,)), ((), ())), preferred_element_type=jnp.float32
    )
    whole_term = (
        first_part
        + lax.dot_general(
            up_local, grad_up, (((1,), (1,)), ((), ())), preferred_element_type=jnp.float32
        )
    ).reshape(model_width, expert_count, tp_count, cap_slots)
    by_block = lax.psum_scatter(
        whole_term.astype(jnp.bfloat16), "tp", scatter_dimension=2, tiled=True
    )
    reduced = lax.psum_scatter(by_block, "etp", scatter_dimension=0, tiled=True).astype(jnp.float32)
    returned = lax.all_to_all(
        reduced.reshape(feat_local, expert_count, cap_slots).astype(jnp.bfloat16),
        "expert",
        split_axis=1,
        concat_axis=1,
        tiled=True,
    ).astype(jnp.float32)
    d_moe = jnp.einsum("tec,dec->td", select, returned, precision=lax.Precision.HIGHEST)
    d_hidden = (d_out.astype(jnp.float32) + d_moe).astype(jnp.bfloat16)
    head_partial = lax.dot_general(
        lax.all_gather(d_hidden, "tp", axis=0, tiled=True),
        w_out,
        (((1,), (1,)), ((), ())),
        preferred_element_type=jnp.float32,
    )
    d_heads = lax.psum_scatter(
        head_partial.astype(jnp.bfloat16), "etp", scatter_dimension=0, tiled=True
    )
    return (d_hidden, d_heads)


def solution(mesh):
    in_specs = (
        P(("expert", "tp"), "etp"),
        P(("expert", "tp"), None),
        P(("expert", "tp"), None),
        P("expert", None, ("etp", "tp")),
        P("expert", None, ("etp", "tp")),
        P("expert", None, ("etp", "tp")),
        P("expert", None, ("etp", "tp")),
        P("expert", ("etp", "tp"), None),
        P("tp", "etp"),
    )
    out_specs = (P(("expert", "tp"), "etp"), P(("expert", "etp"), "tp"))
    return jax.shard_map(body, mesh=mesh, in_specs=in_specs, out_specs=out_specs, check_vma=False)
```

profile of v0, /device:TPU:2, one launch (start us, length us, event | category | flops | bytes accessed | tf_op | source)
XLA Modules:
  0.0 581.8 jit_solution(4109981410665726276)
XLA Ops:
  7.2 0.8 slice_bitcast_fusion.3
  8.3 0.8 slice_bitcast_fusion.1
  9.1 0.2 select_add_fusion
  9.3 0.2 reduce_window_sum.11
  9.7 1.2 convolution_convert_fusion.1
  10.9 13.2 %all_to_all.10 = bf16[4,64,384]{2,1,0:T(8,128)(2,1)S(1)} all-to-all(bf16[4,64,384]{2,1,0:T(8,128)(2,1)S(1)} %convolution_convert_fusion.1), channel_id=1, replica_groups=mesh['expert'=4,'etp'=16,'tp'=4] {'expert'}, dimensions={0} | all-to-all | bytes 393216 | tf_op jit(solution)/shard_map/all_to_all | solution.py:29
  24.1 14.5 %all-gather = bf16[4,256,384]{2,1,0:T(8,128)(2,1)} all-gather(bf16[4,64,384]{2,1,0:T(8,128)(2,1)S(1)} %all_to_all.10), channel_id=2, replica_groups=mesh['expert'=4,'etp'=16,'tp'=4] {'tp'}, dimensions={1}, use_global_device_ids=true | all-gather | bytes 983040 | tf_op jit(solution)/shard_map/all_gather | solution.py:30
  38.7 103.7 %all-gather.3.cloned.1.call-done = bf16[4,4,64,6144]{3,2,1,0:T(8,128)(2,1)} async-done(((bf16[4,4,64,384]{3,2,1,0:T(8,128)(2,1)}), bf16[4,4,64,6144]{3,2,1,0:T(8,128)(2,1)}) %all-gather.3.cloned.1.call-update) | async-done | bytes 12582928 | tf_op jit(solution)/shard_map/all_gather | solution.py:33
  142.4 7.5 %fusion.3 = f32[1024,256]{1,0:T(8,128)S(1)} fusion(bf16[1024,6144]{1,0:T(8,128)(2,1)} %bitcast.60, bf16[1,256,6144]{2,1,0:T(8,128)(2,1)} %param.16), kind=kOutput, calls=%fused_computation.4 | convolution fusion | flops 3221225472 | bytes 16777216 | tf_op jit(solution)/shard_map/dot_general | solution.py:36
  149.9 1.0 copy-done.2
  150.9 10.4 %fusion.1 = f32[1024,6144]{1,0:T(8,128)} fusion(bf16[1,6144,256]{2,1,0:T(8,128)(2,1)S(1)} %copy-done, f32[1024,256]{1,0:T(8,128)S(1)} %fusion.3, bf16[1,1024,256]{2,1,0:T(8,128)(2,1)S(1)} %copy-done.4, bf16[1,1024,256]{2,1,0:T(8,128)(2,1)S(1)} %copy-done.3), kind=kOutput, calls=%fused_computation.2 | convolution fusion | flops 3224371200 | bytes 30408704 | tf_op jit(solution)/shard_map/dot_general | solution.py:46
  161.3 16.2 %add_convert_fusion = bf16[1024,6144]{1,0:T(8,128)(2,1)} fusion(f32[1024,6144]{1,0:T(8,128)} %fusion.1, bf16[1,6144,256]{2,1,0:T(8,128)(2,1)} %param.15, f32[1024,256]{1,0:T(8,128)} %copy-done.2, bf16[1,1024,256]{2,1,0:T(8,128)(2,1)} %param.12), kind=kOutput, calls=%fused_computation | convolution fusion | flops 3235643392 | bytes 42467328 | tf_op jit(solution)/shard_map/dot_general | solution.py:51
  177.5 10.9 %copy.18 = bf16[6144,4,4,64]{0,3,1,2:T(8,128)(2,1)} copy(bf16[6144,4,4,64]{0,3,2,1:T(8,128)(2,1)} %bitcast.55) | data formatting | bytes 25165824 | tf_op jit(solution)/shard_map/convert_element_type | solution.py:56
  188.5 183.0 %reduce-scatter.6.cloned.1.call-done = bf16[6144,4,1,64]{0,3,1,2:T(8,128)(2,1)} async-done(((bf16[6144,4,4,64]{0,3,1,2:T(8,128)(2,1)}), bf16[6144,4,1,64]{0,3,1,2:T(8,128)(2,1)}) %reduce-scatter.6.cloned.1.call-update) | async-done | bytes 3145744 | tf_op jit(solution)/shard_map/reduce_scatter | solution.py:55
  371.4 9.8 %copy.19 = bf16[6144,4,1,64]{3,1,2,0:T(4,128)(2,1)} copy(bf16[6144,4,1,64]{0,3,1,2:T(8,128)(2,1)} %reduce-scatter.6.cloned.1.call-done) | data formatting | bytes 6291456
  381.2 10.0 %reshape.232 = bf16[6144,256]{1,0:T(8,128)(2,1)} reshape(bf16[6144,1,4,64]{3,2,1,0:T(4,128)(2,1)} %bitcast.56) | data formatting | bytes 6291456
  391.3 77.7 %reduce-scatter.10.cloned.1.call-done = bf16[384,256]{1,0:T(8,128)(2,1)} async-done(((bf16[6144,256]{1,0:T(8,128)(2,1)}), bf16[384,256]{1,0:T(8,128)(2,1)}) %reduce-scatter.10.cloned.1.call-update) | async-done | bytes 196624
  469.0 1.2 reshape.233
  470.2 0.9 copy.20
  471.1 11.7 %all_to_all.11 = bf16[384,4,64]{0,2,1:T(8,128)(2,1)S(1)} all-to-all(bf16[384,4,64]{0,2,1:T(8,128)(2,1)} %bitcast.59), channel_id=1, replica_groups=mesh['expert'=4,'etp'=16,'tp'=4] {'expert'}, dimensions={1} | all-to-all | bytes 393216 | tf_op jit(solution)/shard_map/all_to_all | solution.py:59
  482.8 1.1 fusion.6
  483.9 10.0 %all_gather.11 = bf16[512,384]{1,0:T(8,128)(2,1)S(1)} all-gather(bf16[128,384]{1,0:T(8,128)(2,1)S(1)} %fusion.6), channel_id=1, replica_groups=mesh['expert'=4,'etp'=16,'tp'=4] {'tp'}, dimensions={0}, use_global_device_ids=true | all-gather | bytes 491520 | tf_op jit(solution)/shard_map/all_gather | solution.py:69
  494.0 3.4 convolution_convert_fusion
  497.4 77.8 %reduce-scatter.8.cloned.1.call-done = bf16[32,1536]{1,0:T(8,128)(2,1)} async-done(((bf16[512,1536]{1,0:T(8,128)(2,1)}), bf16[32,1536]{1,0:T(8,128)(2,1)}) %reduce-scatter.8.cloned.1.call-update) | async-done | bytes 98320 | tf_op jit(solution)/shard_map/reduce_scatter | solution.py:74
  (25 shorter events, 0.8 us)
Async XLA Ops:
  7.2 143.7 %copy-start = (bf16[1,6144,256]{2,1,0:T(8,128)(2,1)S(1)}, bf16[1,6144,256]{2,1,0:T(8,128)(2,1)}, u32[]{:S(2)}) copy-start(bf16[1,6144,256]{2,1,0:T(8,128)(2,1)} %param.14) | copy-start | bytes 9437188
  7.2 135.2 %all-gather.3.cloned.1.call-start = ((), (), s32[]{:S(2)}) async-start(), calls=%async_computation.5 | async-start | bytes 13369344 | tf_op jit(solution)/shard_map/all_gather | solution.py:33
  38.6 332.8 %reduce-scatter.6.cloned.1.call-start = ((), (), s32[]{:S(2)}) async-start(), calls=%async_computation.6 | async-start | bytes 15728640 | tf_op jit(solution)/shard_map/reduce_scatter | solution.py:55
  142.4 8.5 %copy-start.3 = (bf16[1,1024,256]{2,1,0:T(8,128)(2,1)S(1)}, bf16[1,1024,256]{2,1,0:T(8,128)(2,1)}, u32[]{:S(2)}) copy-start(bf16[1,1024,256]{2,1,0:T(8,128)(2,1)} %param.12) | copy-start | bytes 1572868
  142.4 8.5 %copy-start.4 = (bf16[1,1024,256]{2,1,0:T(8,128)(2,1)S(1)}, bf16[1,1024,256]{2,1,0:T(8,128)(2,1)}, u32[]{:S(2)}) copy-start(bf16[1,1024,256]{2,1,0:T(8,128)(2,1)} %param.13) | copy-start | bytes 1572868
  149.9 1.0 copy-start.2
  188.4 280.6 %reduce-scatter.10.cloned.1.call-start = ((), (), s32[]{:S(2)}) async-start(), calls=%async_computation.8 | async-start | bytes 3342336
  391.3 184.0 %reduce-scatter.8.cloned.1.call-start = ((), (), s32[]{:S(2)}) async-start(), calls=%async_computation.7 | async-start | bytes 1671168 | tf_op jit(solution)/shard_map/reduce_scatter | solution.py:74
  470.1 105.1 %copy-start.1 = (bf16[1,6144,256]{2,1,0:T(8,128)(2,1)S(1)}, bf16[1,6144,256]{2,1,0:T(8,128)(2,1)}, u32[]{:S(2)}) copy-start(bf16[1,6144,256]{2,1,0:T(8,128)(2,1)} %param.14) | copy-start | bytes 9437188
  483.9 91.3 %copy-start.5 = (bf16[128,384]{1,0:T(8,128)(2,1)}, bf16[128,384]{1,0:T(8,128)(2,1)S(1)}, u32[]{:S(2)}) copy-start(bf16[128,384]{1,0:T(8,128)(2,1)S(1)} %fusion.6) | copy-start | bytes 294916
Sparse Core Ops, SparseCore 0:
  38.8 103.5 all-gather.2
  188.5 182.8 reduce-scatter.5
  391.4 77.5 reduce-scatter.9
  497.6 77.6 reduce-scatter.7
where the time goes:
time: 583 us; the launch traced here: 582 us
  waiting for transfers between devices  442 us (76%)
  blocking collectives  49.4 us (8%)
  matrix products  39.9 us (7%)
  local copies, waits for them, and re-layouts  35.6 us (6%)
  between operations  13.9 us (2%)
    reduce_scatter x1, waiting for transfers between devices, body(): lax.psum_scatter(whole_term.astype(jnp.bfloat16), 'tp', scatter_dimension...  183 us
    all_gather x1, waiting for transfers between devices, body(): shard_piece = lax.all_gather(blocks_all, 'etp', axis=3, tiled=True)  104 us
    reduce_scatter x1, waiting for transfers between devices, body(): lax.psum_scatter(head_partial.astype(jnp.bfloat16), 'etp', scatter_dimens...  77.8 us
    unnamed x5, waiting for transfers between devices  77.7 us
    unnamed x16, local copies, waits for them, and re-layouts  22.9 us
    dot_general x1, matrix products, body(): lax.dot_general(up_local, grad_up, (((1,), (1,)), ((), ())), preferred_el...  16.2 us
    all_gather x1, blocking collectives, body(): blocks_all = lax.all_gather(received[:, None], 'tp', axis=1, tiled=True)  14.5 us
    all_to_all x1, blocking collectives, body(): lax.all_to_all(outgoing, 'expert', split_axis=0, concat_axis=0, tiled=True)  13.2 us
  transfers between devices with their start and end apart: 4, of which 4 were waited for; matrix products, arithmetic and copies ran while one was open for 0% of the time, Pallas kernels for 0%

commit v1 on v0

--- a/solution.py
+++ b/solution.py
@@ -2,6 +2,11 @@
 import jax.numpy as jnp
 from jax import lax
 from jax.sharding import PartitionSpec as P
+
+
+def exchange_gather(x, mesh_axis, d):
+    sent = jnp.stack([x] * lax.axis_size(mesh_axis))
+    return jnp.concatenate(lax.all_to_all(sent, mesh_axis, 0, 0), axis=d)
 
 
 def body(d_out, expert_ids, gate_weights, saved_gate, saved_up, w_gate, w_up, w_down, w_out):
@@ -30,7 +35,7 @@
     blocks_all = lax.all_gather(received[:, None], "tp", axis=1, tiled=True)
     down_local = w_down[0]
     slot_rows = blocks_all.shape[0] * blocks_all.shape[1] * blocks_all.shape[2]
-    shard_piece = lax.all_gather(blocks_all, "etp", axis=3, tiled=True)
+    shard_piece = exchange_gather(blocks_all, "etp", 3)
     width_piece = shard_piece.shape[3]
     flat_rows = shard_piece.reshape(slot_rows, width_piece)
     grad_act = lax.dot_general(

time: 583 us -> 643 us (1.10)
  blocking collectives: 49.4 us -> 198 us
  waiting for transfers between devices: 442 us -> 335 us
  local copies, waits for them, and re-layouts: 35.6 us -> 56.1 us
    all_to_all x0 -> x1, blocking collectives: none -> 148 us  [exchange_gather(): return jnp.concatenate(lax.all_to_all(sent, mesh_axis, 0, 0), axis=d)]
    all_gather x1 -> x0, waiting for transfers between devices: 104 us -> none  [body(): shard_piece = lax.all_gather(blocks_all, 'etp', axis=3, tiled=True)]
    reshape x0 -> x1, local copies, waits for them, and re-layouts: none -> 9.09 us  [exchange_gather(): return jnp.concatenate(lax.all_to_all(sent, mesh_axis, 0, 0), axis=d)]
    another operation x0 -> x1, local copies, waits for them, and re-layouts: none -> 7.8 us  [exchange_gather(): sent = jnp.stack([x] * lax.axis_size(mesh_axis))]
    unnamed x16 -> x17, local copies, waits for them, and re-layouts: 22.9 us -> 26.7 us
    unnamed x5 -> x4, waiting for transfers between devices: 77.7 us -> 77.6 us
  transfers between devices with their start and end apart: 4 -> 3, of which waited for: 4 -> 3; matrix products, arithmetic and copies ran while one was open for 0% -> 0% of each run, Pallas kernels for 0% -> 0%
where the time goes in v1:
time: 643 us; the launch traced here: 642 us
  waiting for transfers between devices  335 us (52%)
  blocking collectives  198 us (31%)
  local copies, waits for them, and re-layouts  56.1 us (9%)
  matrix products  37.7 us (6%)
  between operations  13.9 us (2%)
    reduce_scatter x1, waiting for transfers between devices, body(): lax.psum_scatter(whole_term.astype(jnp.bfloat16), 'tp', scatter_dimension...  180 us
    all_to_all x1, blocking collectives, exchange_gather(): return jnp.concatenate(lax.all_to_all(sent, mesh_axis, 0, 0), axis=d)  148 us
    reduce_scatter x1, waiting for transfers between devices, body(): lax.psum_scatter(head_partial.astype(jnp.bfloat16), 'etp', scatter_dimens...  77.7 us
    unnamed x4, waiting for transfers between devices  77.6 us
    unnamed x17, local copies, waits for them, and re-layouts  26.7 us
    dot_general x1, matrix products, body(): lax.dot_general(up_local, grad_up, (((1,), (1,)), ((), ())), preferred_el...  16.2 us
    all_gather x1, blocking collectives, body(): blocks_all = lax.all_gather(received[:, None], 'tp', axis=1, tiled=True)  14.5 us
    all_to_all x1, blocking collectives, body(): lax.all_to_all(outgoing, 'expert', split_axis=0, concat_axis=0, tiled=True)  13.2 us
  transfers between devices with their start and end apart: 3, of which 3 were waited for; matrix products, arithmetic and copies ran while one was open for 0% of the time, Pallas kernels for 0%

profile of v1, /device:TPU:2, one launch (start us, length us, event | category | flops | bytes accessed | tf_op | source)
XLA Modules:
  0.0 641.9 jit_solution(16197531364429572122)
XLA Ops:
  7.2 0.8 slice_bitcast_fusion.3
  9.7 1.2 convolution_convert_fusion.1
  10.9 13.2 %all_to_all.15 = bf16[4,64,384]{2,1,0:T(8,128)(2,1)S(1)} all-to-all(bf16[4,64,384]{2,1,0:T(8,128)(2,1)S(1)} %convolution_convert_fusion.1), channel_id=1, replica_groups=mesh['expert'=4,'etp'=16,'tp'=4] {'expert'}, dimensions={0} | all-to-all | bytes 393216 | tf_op jit(solution)/shard_map/all_to_all | solution.py:34
  24.1 14.5 %all-gather = bf16[4,256,384]{2,1,0:T(8,128)(2,1)} all-gather(bf16[4,64,384]{2,1,0:T(8,128)(2,1)S(1)} %all_to_all.15), channel_id=2, replica_groups=mesh['expert'=4,'etp'=16,'tp'=4] {'tp'}, dimensions={1}, use_global_device_ids=true | all-gather | bytes 983040 | tf_op jit(solution)/shard_map/all_gather | solution.py:35
  38.6 7.8 %stack.2 = bf16[16,4,4,64,384]{4,3,2,1,0:T(8,128)(2,1)} broadcast(bf16[4,4,64,384]{3,2,1,0:T(8,128)(2,1)} %bitcast.63), dimensions={1,2,3,4} | broadcast | bytes 13369344 | tf_op jit(solution)/shard_map/stack | solution.py:8
  46.4 148.4 %all_to_all.16 = bf16[16,4,4,64,384]{4,3,2,1,0:T(8,128)(2,1)S(1)} all-to-all(bf16[16,4,4,64,384]{4,3,2,1,0:T(8,128)(2,1)} %stack.2), channel_id=1, replica_groups=mesh['expert'=4,'etp'=16,'tp'=4] {'etp'}, dimensions={0} | all-to-all | bytes 25165824 | tf_op jit(solution)/shard_map/all_to_all | solution.py:9
  194.8 9.1 %copy.22 = bf16[4,4,64,16,384]{4,3,2,1,0:T(8,128)(2,1)S(1)} copy(bf16[4,4,64,16,384]{4,2,1,0,3:T(8,128)(2,1)S(1)} %bitcast.59) | data formatting | bytes 25165824 | tf_op jit(solution)/shard_map/reshape | solution.py:9
  203.9 3.8 copy.26
  207.7 5.4 fusion.3
  213.2 1.0 copy-done.2
  214.1 10.3 %fusion.1 = f32[1024,6144]{1,0:T(8,128)} fusion(bf16[1,6144,256]{2,1,0:T(8,128)(2,1)S(1)} %copy-done, f32[1024,256]{1,0:T(8,128)S(1)} %fusion.3, bf16[1,1024,256]{2,1,0:T(8,128)(2,1)S(1)} %copy-done.4, bf16[1,1024,256]{2,1,0:T(8,128)(2,1)S(1)} %copy-done.3), kind=kOutput, calls=%fused_computation.2 | convolution fusion | flops 3224371200 | bytes 30408704 | tf_op jit(solution)/shard_map/dot_general | solution.py:51
  224.4 16.2 %add_convert_fusion = bf16[1024,6144]{1,0:T(8,128)(2,1)} fusion(f32[1024,6144]{1,0:T(8,128)} %fusion.1, bf16[1,6144,256]{2,1,0:T(8,128)(2,1)} %param.15, f32[1024,256]{1,0:T(8,128)} %copy-done.2, bf16[1,1024,256]{2,1,0:T(8,128)(2,1)} %param.12), kind=kOutput, calls=%fused_computation | convolution fusion | flops 3235643392 | bytes 42467328 | tf_op jit(solution)/shard_map/dot_general | solution.py:56
  240.7 10.7 %copy.23 = bf16[6144,4,4,64]{0,3,1,2:T(8,128)(2,1)} copy(bf16[6144,4,4,64]{0,3,2,1:T(8,128)(2,1)} %bitcast.58) | data formatting | bytes 25165824 | tf_op jit(solution)/shard_map/convert_element_type | solution.py:61
  251.6 180.2 %reduce-scatter.6.cloned.1.call-done = bf16[6144,4,1,64]{0,3,1,2:T(8,128)(2,1)} async-done(((bf16[6144,4,4,64]{0,3,1,2:T(8,128)(2,1)}), bf16[6144,4,1,64]{0,3,1,2:T(8,128)(2,1)}) %reduce-scatter.6.cloned.1.call-update) | async-done | bytes 3145744 | tf_op jit(solution)/shard_map/reduce_scatter | solution.py:60
  431.8 9.8 %copy.24 = bf16[6144,4,1,64]{3,1,2,0:T(4,128)(2,1)} copy(bf16[6144,4,1,64]{0,3,1,2:T(8,128)(2,1)} %reduce-scatter.6.cloned.1.call-done) | data formatting | bytes 6291456
  441.6 10.0 %reshape.234 = bf16[6144,256]{1,0:T(8,128)(2,1)} reshape(bf16[6144,1,4,64]{3,2,1,0:T(4,128)(2,1)} %bitcast.61) | data formatting | bytes 6291456
  451.7 77.5 %reduce-scatter.10.cloned.1.call-done = bf16[384,256]{1,0:T(8,128)(2,1)} async-done(((bf16[6144,256]{1,0:T(8,128)(2,1)}), bf16[384,256]{1,0:T(8,128)(2,1)}) %reduce-scatter.10.cloned.1.call-update) | async-done | bytes 196624
  529.2 1.2 reshape.235
  530.4 0.9 copy.25
  531.3 11.7 %all_to_all.17 = bf16[384,4,64]{0,2,1:T(8,128)(2,1)S(1)} all-to-all(bf16[384,4,64]{0,2,1:T(8,128)(2,1)} %bitcast.65), channel_id=1, replica_groups=mesh['expert'=4,'etp'=16,'tp'=4] {'expert'}, dimensions={1} | all-to-all | bytes 393216 | tf_op jit(solution)/shard_map/all_to_all | solution.py:64
  543.1 1.1 fusion.6
  544.2 10.0 %all_gather.7 = bf16[512,384]{1,0:T(8,128)(2,1)S(1)} all-gather(bf16[128,384]{1,0:T(8,128)(2,1)S(1)} %fusion.6), channel_id=1, replica_groups=mesh['expert'=4,'etp'=16,'tp'=4] {'tp'}, dimensions={0}, use_global_device_ids=true | all-gather | bytes 491520 | tf_op jit(solution)/shard_map/all_gather | solution.py:74
  554.2 3.4 convolution_convert_fusion
  557.7 77.7 %reduce-scatter.8.cloned.1.call-done = bf16[32,1536]{1,0:T(8,128)(2,1)} async-done(((bf16[512,1536]{1,0:T(8,128)(2,1)}), bf16[32,1536]{1,0:T(8,128)(2,1)}) %reduce-scatter.8.cloned.1.call-update) | async-done | bytes 98320 | tf_op jit(solution)/shard_map/reduce_scatter | solution.py:79
  (26 shorter events, 2.0 us)
Async XLA Ops:
  7.2 207.0 %copy-start = (bf16[1,6144,256]{2,1,0:T(8,128)(2,1)S(1)}, bf16[1,6144,256]{2,1,0:T(8,128)(2,1)}, u32[]{:S(2)}) copy-start(bf16[1,6144,256]{2,1,0:T(8,128)(2,1)} %param.14) | copy-start | bytes 9437188
  7.2 424.7 %reduce-scatter.6.cloned.1.call-start = ((), (), s32[]{:S(2)}) async-start(), calls=%async_computation.6 | async-start | bytes 15728640 | tf_op jit(solution)/shard_map/reduce_scatter | solution.py:60
  207.7 6.4 %copy-start.3 = (bf16[1,1024,256]{2,1,0:T(8,128)(2,1)S(1)}, bf16[1,1024,256]{2,1,0:T(8,128)(2,1)}, u32[]{:S(2)}) copy-start(bf16[1,1024,256]{2,1,0:T(8,128)(2,1)} %param.12) | copy-start | bytes 1572868
  207.7 6.4 %copy-start.4 = (bf16[1,1024,256]{2,1,0:T(8,128)(2,1)S(1)}, bf16[1,1024,256]{2,1,0:T(8,128)(2,1)}, u32[]{:S(2)}) copy-start(bf16[1,1024,256]{2,1,0:T(8,128)(2,1)} %param.13) | copy-start | bytes 1572868
  213.2 1.0 copy-start.2
  251.4 277.8 %reduce-scatter.10.cloned.1.call-start = ((), (), s32[]{:S(2)}) async-start(), calls=%async_computation.8 | async-start | bytes 3342336
  451.7 183.7 %reduce-scatter.8.cloned.1.call-start = ((), (), s32[]{:S(2)}) async-start(), calls=%async_computation.7 | async-start | bytes 1671168 | tf_op jit(solution)/shard_map/reduce_scatter | solution.py:79
  530.4 105.0 %copy-start.1 = (bf16[1,6144,256]{2,1,0:T(8,128)(2,1)S(1)}, bf16[1,6144,256]{2,1,0:T(8,128)(2,1)}, u32[]{:S(2)}) copy-start(bf16[1,6144,256]{2,1,0:T(8,128)(2,1)} %param.14) | copy-start | bytes 9437188
  544.2 91.2 %copy-start.5 = (bf16[128,384]{1,0:T(8,128)(2,1)}, bf16[128,384]{1,0:T(8,128)(2,1)S(1)}, u32[]{:S(2)}) copy-start(bf16[128,384]{1,0:T(8,128)(2,1)S(1)} %fusion.6) | copy-start | bytes 294916
Sparse Core Ops, SparseCore 0:
  251.5 180.2 reduce-scatter.5
  451.8 77.3 reduce-scatter.9
  557.8 77.5 reduce-scatter.7
